TPU v7x, 128 devices: a whole 4x4x4 slice. The times are simulated.
128 devices in a mesh: context: 8 (over z, core), tensor: 16 (over x, y).
Axes of the slice: x: 4, y: 4, z: 4, core: 2. Of those that a mesh axis runs over, the one named last changes fastest.
Arguments:
- features: bfloat16 [4096, 3, 8192], P('context', None, 'tensor'), may hold values from -6 to 6
- se_filter: float32 [7, 3, 8192], P(None, None, 'tensor'), may hold values from -1.6 to 1.6
- mr_filter: bfloat16 [128, 512], P(None, 'tensor'), may hold values from -0.61 to 0.61
- stream: bfloat16 [4096, 8192], P('context', 'tensor'), may hold values from -20 to 20
- w_out: bfloat16 [8192, 8192], P('tensor'), may hold values from -0.09375 to 0.09375
- norm_gain: float32 [8192], replicated, may hold values from 0.1 to 1.9
- w_qkv: bfloat16 [8192, 3, 4096], P(None, None, 'tensor'), as said below
Outputs:
- stream_out: bfloat16 [4096, 8192], P('context', 'tensor')
- context_out: bfloat16 [4096, 4096], P('context', 'tensor')
Inputs may be any that keep to these rules, and one draw needn't show every extreme that they name: `w_qkv`: projection weights.
All inputs are finite; a program needn't handle non-finite values.
Results may differ from a plain program's by a relative error of at most 0.019.
Values may be sent and summed in bfloat16 or wider, within the bound.
No kernel may reach another device: no remote copies, remote signals or barrier semaphores. Data moves between devices by JAX's collectives and lax.ppermute only.
A program may use at most 192 MiB of HBM per device.

v0:
```python
import jax
import jax.numpy as jnp
from jax import lax
from jax.sharding import PartitionSpec as P

HD = 128


def passed_along(value, axis, steps):
    count = lax.axis_size(axis)
    initial, last = (max(0, -steps), min(count, count - steps))
    return lax.ppermute(value, axis, [(source, source + steps) for source in range(initial, last)])


def short_filter(padded, se_filter, row_count):
    se_width = se_filter.shape[0]
    filtered = se_filter[0][None] * padded[se_width - 1 : se_width - 1 + row_count].astype(
        jnp.float32
    )
    for offset_lag in range(1, se_width):
        window = padded[se_width - 1 - offset_lag : se_width - 1 - offset_lag + row_count].astype(
            jnp.float32
        )
        filtered = filtered + se_filter[offset_lag][None] * window
    return filtered


def toeplitz_blocks(mr_filter):
    blocks = mr_filter.shape[0]
    groups = mr_filter.shape[1]
    reversed_taps = mr_filter[::-1].T
    period_row = jnp.concatenate([reversed_taps, jnp.zeros((groups, blocks), jnp.bfloat16)], axis=1)
    tiled = jnp.tile(period_row, (1, blocks))[:, : blocks * (2 * blocks - 1)]
    tiled = tiled.reshape(groups, blocks, 2 * blocks - 1)
    return jnp.concatenate([tiled, jnp.zeros((groups, blocks, 1), jnp.bfloat16)], axis=2)


def medium_filter(kv_prev, kv_prod, mr_filter):
    tok_rows, own_chans = kv_prod.shape
    blocks = mr_filter.shape[0]
    groups = mr_filter.shape[1]
    group_width = own_chans // groups
    block_count = tok_rows // blocks
    extended = jnp.concatenate([kv_prev, kv_prod, jnp.zeros((1, own_chans), jnp.bfloat16)], axis=0)
    lower = extended[:tok_rows].reshape(block_count, blocks, groups, group_width)
    upper = extended[blocks : blocks + tok_rows].reshape(block_count, blocks, groups, group_width)
    toeplitz = toeplitz_blocks(mr_filter)
    medium = jnp.einsum(
        "gim,bmgc->bigc", toeplitz[:, :, :blocks], lower, preferred_element_type=jnp.float32
    )
    medium = medium + jnp.einsum(
        "gim,bmgc->bigc", toeplitz[:, :, blocks:], upper, preferred_element_type=jnp.float32
    )
    return medium.reshape(tok_rows, own_chans)


def on_device(features, se_filter, mr_filter, stream, w_out, norm_gain, w_qkv):
    tok_rows = features.shape[0]
    own_chans = features.shape[2]
    se_width = se_filter.shape[0]
    mr_width = mr_filter.shape[0]
    edge_rows = passed_along(features[tok_rows - (se_width - 1) :], "context", 1)
    short_out = short_filter(jnp.concatenate([edge_rows, features], axis=0), se_filter, tok_rows)
    kv_prod = (short_out[:, 1, :] * short_out[:, 2, :]).astype(jnp.bfloat16)
    kv_prev = passed_along(kv_prod[tok_rows - (mr_width - 1) :], "context", 1)
    medium = medium_filter(kv_prev, kv_prod, mr_filter)
    gated = (short_out[:, 0, :] * medium).astype(jnp.bfloat16)
    tensor_rank = lax.axis_index("tensor")
    partial_value = jnp.dot(gated, w_out, preferred_element_type=jnp.float32)
    own_cols = lax.dynamic_slice_in_dim(
        partial_value, tensor_rank * own_chans, own_chans, 1
    ) + stream.astype(jnp.float32)
    term_all = lax.dynamic_update_slice_in_dim(partial_value, own_cols, tensor_rank * own_chans, 1)
    mixed_rows = lax.psum(term_all, "tensor")
    stream_out = lax.dynamic_slice_in_dim(mixed_rows, tensor_rank * own_chans, own_chans, 1).astype(
        jnp.bfloat16
    )
    mean_square = jnp.mean(mixed_rows * mixed_rows, axis=1, keepdims=True)
    normed = (mixed_rows * lax.rsqrt(mean_square + 1e-05) * norm_gain[None, :]).astype(jnp.bfloat16)
    qkv_proj = jnp.einsum("td,dkh->tkh", normed, w_qkv, preferred_element_type=jnp.float32).astype(
        jnp.bfloat16
    )
    head_cols = w_qkv.shape[2]
    head_count = head_cols // HD
    query = qkv_proj[:, 0, :].reshape(tok_rows, head_count, HD)
    position = lax.axis_index("context") * tok_rows + jnp.arange(tok_rows, dtype=jnp.int32)
    scale_factor = HD ** (-0.5)
    run_max = jnp.full((head_count, tok_rows), -1e30, jnp.float32)
    key_block = lax.all_gather(qkv_proj[:, 1, :], "context", axis=0, tiled=True)
    value_block = lax.all_gather(qkv_proj[:, 2, :], "context", axis=0, tiled=True)
    key_count = key_block.shape[0]
    keys_three = key_block.reshape(key_count, head_count, HD)
    values_three = value_block.reshape(key_count, head_count, HD)
    scores = (
        jnp.einsum("qhd,khd->hqk", query, keys_three, preferred_element_type=jnp.float32)
        * scale_factor
    )
    key_position = jnp.arange(key_count, dtype=jnp.int32)
    allowed = key_position[None, :] <= position[:, None]
    scores = jnp.where(allowed[None], scores, -jnp.inf)
    new_max = jnp.maximum(run_max, jnp.max(scores, axis=2))
    expo = jnp.exp(scores - new_max[:, :, None])
    run_total = jnp.sum(expo, axis=2)
    weights = expo.astype(jnp.bfloat16)
    run_acc = jnp.einsum("hqk,khd->hqd", weights, values_three, preferred_element_type=jnp.float32)
    run_max, run_total, run_acc = (new_max, run_total, run_acc)
    result = run_acc / run_total[:, :, None]
    context_out = jnp.transpose(result, (1, 0, 2)).reshape(tok_rows, head_cols).astype(jnp.bfloat16)
    return (stream_out, context_out)


def solution(mesh):
    placed = (
        P("context", None, "tensor"),
        P(None, None, "tensor"),
        P(None, "tensor"),
        P("context", "tensor"),
        P("tensor", None),
        P(),
        P(None, None, "tensor"),
    )
    return jax.shard_map(
        on_device,
        mesh=mesh,
        in_specs=placed,
        out_specs=(P("context", "tensor"), P("context", "tensor")),
        check_vma=False,
    )
```

profile of v0, /device:TPU:1, one launch (start us, length us, event | category | flops | bytes accessed | tf_op | source)
XLA Modules:
  0.0 383.0 jit_solution(14725790758552800340)
XLA Ops:
  7.2 0.7 slice.85
  8.2 4.9 %collective-permute-start = (bf16[6,3,512]{0,2,1:T(8,128)(2,1)S(1)}, bf16[6,3,512]{0,2,1:T(8,128)(2,1)S(1)}, u32[]{:S(2)}, u32[]{:S(2)}) collective-permute-start(bf16[6,3,512]{0,2,1:T(8,128)(2,1)S(1)} %copy.14), channel_id=1, source_target_pairs={{0,16},{16,32},{32,48},{48,64},{64,80},{80,96},{96,112},{1,17},{17... | collective-permute-start | bytes 55304 | tf_op jit(solution)/shard_map/ppermute | solution.py:12
  13.2 1.2 fusion.42
  14.4 0.6 copy_bitcast_fusion.2
  15.0 0.6 copy_bitcast_fusion.4
  15.6 2.6 copy.13
  18.5 1.2 copy.35
  19.8 7.8 %reshape.68 = bf16[32,128,255]{2,1,0:T(8,128)(2,1)} reshape(bf16[32,32640]{1,0:T(8,128)(2,1)S(1)} %slice.124) | data formatting | bytes 4177920 | tf_op jit(solution)/shard_map/reshape | solution.py:34
  28.2 12.6 %multiply_add_fusion = f32[512,3,512]{0,2,1:T(8,128)S(1)} fusion(bf16[512,3,512]{0,2,1:T(8,128)(2,1)} %copy.13, bf16[6,3,512]{0,2,1:T(8,128)(2,1)S(1)} %collective-permute-done, f32[3,512]{1,0:T(4,128)S(1)} %get-tuple-element.20, f32[3,512]{1,0:T(4,128)S(1)} %get-tuple-element.21, f32[3,512]{1,0:T(4,128)} %get-tuple-element.22, ...), kind=kLoop, calls=%fused_computation.19 | loop fusion | flops 29884416 | bytes 4780032 | tf_op jit(solution)/shard_map/add | solution.py:24
  41.1 1.9 collective-permute-start.1
  43.2 1.8 collective-permute-done.1
  44.9 1.5 pad_maximum_fusion.1
  46.4 2.0 reshape.69
  48.4 2.0 reshape.67
  50.4 2.3 fusion.24
  52.7 0.8 fusion.19
  54.0 11.6 %fusion.34 = f32[512,8192]{1,0:T(8,128)} fusion(bf16[512,8192]{1,0:T(8,128)(2,1)} %param.11, f32[64,8,4,128]{3,2,1,0:T(4,128)S(1)} %bitcast.73, f32[512,3,512]{0,2,1:T(8,128)S(1)} %multiply_add_fusion), kind=kOutput, calls=%fused_computation.49 | convolution fusion | flops 4295491584 | bytes 27262976 | tf_op jit(solution)/shard_map/dot_general | solution.py:69
  65.6 2.4 add_dynamic-update-slice_fusion
  68.2 222.7 %all-reduce.5.cloned.1.call-done = f32[512,8192]{1,0:T(8,128)} async-done(((f32[512,8192]{1,0:T(8,128)}), f32[512,8192]{1,0:T(8,128)}) %all-reduce.5.cloned.1.call-update) | async-done | bytes 16777232 | tf_op jit(solution)/shard_map/psum | solution.py:74
  290.9 7.0 %multiply_reduce_fusion = f32[512]{0:T(512)S(1)} fusion(f32[512,8192]{1,0:T(8,128)} %all-reduce.5.cloned.1.call-done), kind=kLoop, calls=%fused_computation.3 | loop fusion | flops 8388096 | bytes 16779264 | tf_op jit(solution)/shard_map/reduce_sum | solution.py:78
  297.9 14.8 %fusion.16 = bf16[512,3,256]{0,2,1:T(8,128)(2,1)S(1)} fusion(bf16[8192,3,256]{2,0,1:T(8,128)(2,1)} %param.13, f32[512,8192]{1,0:T(8,128)} %all-reduce.5.cloned.1.call-done, f32[8192]{0:T(1024)S(1)} %copy-done.5, f32[512]{0:T(512)S(1)} %add_rsqrt_fusion), kind=kOutput, calls=%fused_computation.32 | convolution fusion | flops 6455427072 | bytes 30181376 | tf_op jit(solution)/shard_map/td,dkh->tkh/dot_general | solution.py:80
  312.7 0.8 fusion.41
  313.6 0.7 all-gather.7.cloned.1.call-update
  314.3 1.7 iota_compare_fusion
  316.0 2.1 dynamic-slice_convert_fusion
  318.1 21.7 %all-gather.5.cloned.1.call-done = bf16[4096,1,256]{0,2,1:T(8,128)(2,1)} async-done(((bf16[512,1,256]{0,2,1:T(8,128)(2,1)}), bf16[4096,1,256]{0,2,1:T(8,128)(2,1)}) %all-gather.5.cloned.1.call-update) | async-done | bytes 2097168 | tf_op jit(solution)/shard_map/all_gather | solution.py:89
  339.7 5.3 %fusion = (f32[2,512]{1,0:T(2,128)S(1)}, f32[2,512,4096]{2,1,0:T(8,128)S(1)}) fusion(pred[512,4096]{1,0:T(8,128)(4,1)S(1)} %iota_compare_fusion, bf16[512,2,128]{0,2,1:T(8,128)(2,1)S(1)} %bitcast.77, bf16[4096,2,128]{0,2,1:T(8,128)(2,1)} %bitcast.81), kind=kOutput, calls=%fused_computation.4 | convolution fusion | flops 1086323712 | bytes 21237760 | tf_op jit(solution)/shard_map/qhd,khd->hqk/dot_general | solution.py:95
  345.1 5.7 %copy-done = f32[2,512,4096]{2,1,0:T(8,128)} copy-done((f32[2,512,4096]{2,1,0:T(8,128)}, f32[2,512,4096]{2,1,0:T(8,128)S(1)}, u32[]{:S(2)}) %copy-start) | copy-done | bytes 16777240
  350.8 4.6 %fusion.1 = f32[2,512]{1,0:T(2,128)S(1)} fusion(f32[2,512,4096]{2,1,0:T(8,128)S(1)} %get-tuple-element.19, f32[2,512]{1,0:T(2,128)S(1)} %broadcast_maximum_fusion, pred[512,4096]{1,0:T(8,128)(4,1)S(1)} %iota_compare_fusion), kind=kLoop, calls=%fused_computation.5 | loop fusion | flops 16776192 | bytes 18882560 | tf_op jit(solution)/shard_map/reduce_sum | solution.py:103
  355.4 11.9 %all-gather.7.cloned.1.call-done = bf16[4096,1,256]{0,2,1:T(8,128)(2,1)} async-done(((bf16[512,1,256]{0,2,1:T(8,128)(2,1)}), bf16[4096,1,256]{0,2,1:T(8,128)(2,1)}) %all-gather.7.cloned.1.call-update) | async-done | bytes 2097168 | tf_op jit(solution)/shard_map/all_gather | solution.py:90
  367.2 8.4 %fusion.31 = bf16[512,2,128]{0,2,1:T(8,128)(2,1)S(1)} fusion(bf16[4096,2,128]{0,2,1:T(8,128)(2,1)} %bitcast.82, f32[2,512,4096]{2,1,0:T(8,128)} %copy-done, f32[2,512]{1,0:T(2,128)S(1)} %broadcast_maximum_fusion, pred[512,4096]{1,0:T(8,128)(4,1)S(1)} %iota_compare_fusion, f32[512,2]{0,1:T(2,128)S(1)} %bitcast.80), kind=kOutput, calls=%fused_computation.47 | convolution fusion | flops 1090781184 | bytes 21241856 | tf_op jit(solution)/shard_map/hqk,khd->hqd/dot_general | solution.py:105
  375.7 0.8 copy.22
  (31 shorter events, 2.5 us)
Async XLA Ops:
  7.2 11.1 %copy-start.4 = (bf16[128,32]{0,1:T(8,128)(2,1)S(1)}, bf16[128,32]{0,1:T(8,128)(2,1)}, u32[]{:S(2)}) copy-start(bf16[128,32]{0,1:T(8,128)(2,1)} %param.9) | copy-start | bytes 24580
  7.2 283.8 %all-reduce.5.cloned.1.call-start = ((), (), s32[]{:S(2)}) async-start(), calls=%async_computation | async-start | bytes 33554432 | tf_op jit(solution)/shard_map/psum | solution.py:74
  8.2 20.0 %collective-permute-start = (bf16[6,3,512]{0,2,1:T(8,128)(2,1)S(1)}, bf16[6,3,512]{0,2,1:T(8,128)(2,1)S(1)}, u32[]{:S(2)}, u32[]{:S(2)}) collective-permute-start(bf16[6,3,512]{0,2,1:T(8,128)(2,1)S(1)} %copy.14), channel_id=1, source_target_pairs={{0,16},{16,32},{32,48},{48,64},{64,80},{80,96},{96,112},{1,17},{17... | collective-permute-start | bytes 55304 | tf_op jit(solution)/shard_map/ppermute | solution.py:12
  41.1 3.9 %collective-permute-start.1 = (bf16[127,512]{0,1:T(8,128)(2,1)S(1)}, bf16[127,512]{0,1:T(8,128)(2,1)S(1)}, u32[]{:S(2)}, u32[]{:S(2)}) collective-permute-start(bf16[127,512]{0,1:T(8,128)(2,1)S(1)} %slice_bitcast_fusion.3), channel_id=1, source_target_pairs={{0,16},{16,32},{32,48},{48,64},{64,80},{80,96},{96,112},{1,17},{17... | collective-permute-start | bytes 390152 | tf_op jit(solution)/shard_map/ppermute | solution.py:12
  50.4 2.3 copy-start.1
  50.4 2.4 copy-start.2
  54.0 11.6 %copy-start.3 = (bf16[512,512]{1,0:T(8,128)(2,1)S(1)}, bf16[512,512]{1,0:T(8,128)(2,1)}, u32[]{:S(2)}) copy-start(bf16[512,512]{1,0:T(8,128)(2,1)} %param.10) | copy-start | bytes 1572868
  68.0 229.9 %copy-start.5 = (f32[8192]{0:T(1024)S(1)}, f32[8192]{0:T(1024)}, u32[]{:S(2)}) copy-start(f32[8192]{0:T(1024)} %param.12) | copy-start | bytes 98308
  68.0 271.8 %all-gather.5.cloned.1.call-start = ((), (), s32[]{:S(2)}) async-start(), calls=%async_computation.1 | async-start | bytes 2359296 | tf_op jit(solution)/shard_map/all_gather | solution.py:89
  313.6 53.7 %all-gather.7.cloned.1.call-start = ((), (), s32[]{:S(2)}) async-start(), calls=%async_computation.2 | async-start | bytes 2359296 | tf_op jit(solution)/shard_map/all_gather | solution.py:90
  345.0 5.7 %copy-start = (f32[2,512,4096]{2,1,0:T(8,128)}, f32[2,512,4096]{2,1,0:T(8,128)S(1)}, u32[]{:S(2)}) copy-start(f32[2,512,4096]{2,1,0:T(8,128)S(1)} %get-tuple-element.19) | copy-start | bytes 50331652
Sparse Core Ops, SparseCore 0:
  68.1 222.7 all-reduce.4
  313.7 26.0 all-gather.4
  341.4 25.7 all-gather.6
where the time goes:
time: 384 us; the launch traced here: 383 us
  waiting for transfers between devices  259 us (67%)
  matrix products  43.2 us (11%)
  local copies, waits for them, and re-layouts  30 us (8%)
  other arithmetic  30 us (8%)
  between operations  13.9 us (4%)
  starting transfers between devices  7.16 us (2%)
    psum x1, waiting for transfers between devices, on_device(): mixed_rows = lax.psum(term_all, 'tensor')  223 us
    all_gather x1, waiting for transfers between devices, on_device(): key_block = lax.all_gather(qkv_proj[:, 1, :], 'context', axis=0, tiled=True)  21.7 us
    dot_general x1, matrix products, on_device(): jnp.einsum('td,dkh->tkh', normed, w_qkv, preferred_element_type=jnp.float32)  14.8 us
    add x1, other arithmetic, short_filter(): filtered = filtered + se_filter[offset_lag][None] * window  12.6 us
    unnamed x19, local copies, waits for them, and re-layouts  12.2 us
    all_gather x1, waiting for transfers between devices, on_device(): lax.all_gather(qkv_proj[:, 2, :], 'context', axis=0, tiled=True)  11.9 us
    dot_general x1, matrix products, on_device(): partial_value = jnp.dot(gated, w_out, preferred_element_type=jnp.float32)  11.6 us
    dot_general x1, matrix products, on_device(): jnp.einsum('hqk,khd->hqd', weights, values_three, preferred_element_type=...  8.42 us
  transfers between devices with their start and end apart: 5, of which 4 were waited for; matrix products, arithmetic and copies ran while one was open for 8% of the time, Pallas kernels for 0%

commit v1 on v0

--- a/solution.py
+++ b/solution.py
@@ -71,7 +71,11 @@
         partial_value, tensor_rank * own_chans, own_chans, 1
     ) + stream.astype(jnp.float32)
     term_all = lax.dynamic_update_slice_in_dim(partial_value, own_cols, tensor_rank * own_chans, 1)
-    mixed_rows = lax.psum(term_all, "tensor")
+    mixed_rows = term_all
+    for hop in (1, 2, 4, 8):
+        mixed_rows = mixed_rows + lax.ppermute(
+            mixed_rows, "tensor", [(dev, dev ^ hop) for dev in range(16)]
+        )
     stream_out = lax.dynamic_slice_in_dim(mixed_rows, tensor_rank * own_chans, own_chans, 1).astype(
         jnp.bfloat16
     )

time: 384 us -> 1640 us (4.27)
  waiting for transfers between devices: 259 us -> 1480 us
  other arithmetic: 30 us -> 67.4 us
    ppermute x0 -> x4, waiting for transfers between devices: none -> 1440 us  [on_device(): lax.ppermute(mixed_rows, 'tensor', [(dev, dev ^ hop) for dev in range(16)])]
    psum x1 -> x0, waiting for transfers between devices: 223 us -> none  [on_device(): mixed_rows = lax.psum(term_all, 'tensor')]
    add x0 -> x3, other arithmetic: none -> 34.8 us  [on_device(): mixed_rows + lax.ppermute(mixed_rows, 'tensor', [(dev, dev ^ hop) for dev...]
  transfers between devices with their start and end apart: 5 -> 8, of which waited for: 4 -> 7; matrix products, arithmetic and copies ran while one was open for 8% -> 2% of each run, Pallas kernels for 0% -> 0%
where the time goes in v1:
time: 1640 us
  waiting for transfers between devices  1480 us (90%)
  other arithmetic  67.4 us (4%)
  matrix products  38.8 us (2%)
  local copies, waits for them, and re-layouts  30 us (2%)
    ppermute x4, waiting for transfers between devices, on_device(): lax.ppermute(mixed_rows, 'tensor', [(dev, dev ^ hop) for dev in range(16)])  1440 us
    add x3, other arithmetic, on_device(): mixed_rows + lax.ppermute(mixed_rows, 'tensor', [(dev, dev ^ hop) for dev...  34.8 us
  transfers between devices with their start and end apart: 8, of which 7 were waited for; matrix products, arithmetic and copies ran while one was open for 2% of the time, Pallas kernels for 0%

profile of v1, /device:TPU:1, one launch (start us, length us, event | category | flops | bytes accessed | tf_op | source)
XLA Modules:
  0.0 1642.0 jit_solution(11948876182535776036)
XLA Ops:
  8.2 4.9 collective-permute-start
  15.6 2.6 copy.13
  20.4 7.8 reshape.68
  28.2 12.4 multiply_add_fusion
  40.8 1.9 collective-permute-start.1
  42.9 1.8 collective-permute-done.1
  44.7 1.5 pad_maximum_fusion.1
  46.1 2.0 reshape.69
  48.1 2.0 reshape.67
  50.1 2.3 fusion.24
  53.7 7.2 fusion.34
  61.1 1.4 collective-permute-start.2
  62.5 361.0 %collective-permute-done.2 = f32[512,8192]{1,0:T(8,128)} collective-permute-done((f32[512,8192]{1,0:T(8,128)S(1)}, f32[512,8192]{1,0:T(8,128)}, u32[]{:S(2)}, u32[]{:S(2)}) %collective-permute-start.2) | collective-permute-done | bytes 16777248 | tf_op jit(solution)/shard_map/ppermute | solution.py:76
  423.6 11.7 add.81
  435.3 2.9 collective-permute-start.3
  438.2 360.3 %collective-permute-done.3 = f32[512,8192]{1,0:T(8,128)} collective-permute-done((f32[512,8192]{1,0:T(8,128)}, f32[512,8192]{1,0:T(8,128)}, u32[]{:S(2)}, u32[]{:S(2)}) %collective-permute-start.3) | collective-permute-done | bytes 16777248 | tf_op jit(solution)/shard_map/ppermute | solution.py:76
  798.5 11.3 add.82
  809.8 1.3 collective-permute-start.4
  811.1 359.4 %collective-permute-done.4 = f32[512,8192]{1,0:T(8,128)} collective-permute-done((f32[512,8192]{1,0:T(8,128)S(1)}, f32[512,8192]{1,0:T(8,128)}, u32[]{:S(2)}, u32[]{:S(2)}) %collective-permute-start.4) | collective-permute-done | bytes 16777248 | tf_op jit(solution)/shard_map/ppermute | solution.py:76
  1170.5 11.8 add.83
  1182.3 2.7 collective-permute-start.5
  1185.0 358.5 %collective-permute-done.5 = f32[512,8192]{1,0:T(8,128)S(1)} collective-permute-done((f32[512,8192]{1,0:T(8,128)}, f32[512,8192]{1,0:T(8,128)S(1)}, u32[]{:S(2)}, u32[]{:S(2)}) %collective-permute-start.5) | collective-permute-done | bytes 16777248 | tf_op jit(solution)/shard_map/ppermute | solution.py:76
  1543.5 12.0 multiply_reduce_fusion
  1555.5 14.8 fusion.16
  1572.0 1.7 iota_compare_fusion
  1573.6 2.1 dynamic-slice_convert_fusion
  1575.7 22.7 %all-gather.5.cloned.1.call-done = bf16[4096,1,256]{0,2,1:T(8,128)(2,1)} async-done(((bf16[512,1,256]{0,2,1:T(8,128)(2,1)}), bf16[4096,1,256]{0,2,1:T(8,128)(2,1)}) %all-gather.5.cloned.1.call-update) | async-done | bytes 2097168 | tf_op jit(solution)/shard_map/all_gather | solution.py:93
  1598.5 5.3 fusion
  1603.8 5.7 copy-done
  1609.5 4.6 fusion.1
  1614.1 11.9 all-gather.7.cloned.1.call-done
  1625.9 8.4 fusion.31
  (39 shorter events, 10.0 us)
Async XLA Ops:
  7.2 11.6 copy-start.4
  7.2 1591.3 %all-gather.5.cloned.1.call-start = ((), (), s32[]{:S(2)}) async-start(), calls=%async_computation | async-start | bytes 2359296 | tf_op jit(solution)/shard_map/all_gather | solution.py:93
  8.2 19.9 %collective-permute-start = (bf16[6,3,512]{0,2,1:T(8,128)(2,1)S(1)}, bf16[6,3,512]{0,2,1:T(8,128)(2,1)S(1)}, u32[]{:S(2)}, u32[]{:S(2)}) collective-permute-start(bf16[6,3,512]{0,2,1:T(8,128)(2,1)S(1)} %copy.14), channel_id=1, source_target_pairs={{0,16},{16,32},{32,48},{48,64},{64,80},{80,96},{96,112},{1,17},{17... | collective-permute-start | bytes 55304 | tf_op jit(solution)/shard_map/ppermute | solution.py:12
  40.8 3.9 collective-permute-start.1
  50.1 2.3 copy-start.1
  50.1 2.4 copy-start.2
  53.7 7.2 copy-start.3
  61.1 362.4 %collective-permute-start.2 = (f32[512,8192]{1,0:T(8,128)S(1)}, f32[512,8192]{1,0:T(8,128)}, u32[]{:S(2)}, u32[]{:S(2)}) collective-permute-start(f32[512,8192]{1,0:T(8,128)S(1)} %add_dynamic-update-slice_fusion), channel_id=1, source_target_pairs={{0,1},{1,0},{2,3},{3,2},{4,5},{5,4},{6,7},{7,6},{8,9},{9,8},{10,11... | collective-permute-start | bytes 50331656 | tf_op jit(solution)/shard_map/ppermute | solution.py:76
  435.3 363.2 %collective-permute-start.3 = (f32[512,8192]{1,0:T(8,128)}, f32[512,8192]{1,0:T(8,128)}, u32[]{:S(2)}, u32[]{:S(2)}) collective-permute-start(f32[512,8192]{1,0:T(8,128)} %add.81), channel_id=1, source_target_pairs={{0,2},{1,3},{2,0},{3,1},{4,6},{5,7},{6,4},{7,5},{8,10},{9,11},{10,... | collective-permute-start | bytes 50331656 | tf_op jit(solution)/shard_map/ppermute | solution.py:76
  809.8 360.7 %collective-permute-start.4 = (f32[512,8192]{1,0:T(8,128)S(1)}, f32[512,8192]{1,0:T(8,128)}, u32[]{:S(2)}, u32[]{:S(2)}) collective-permute-start(f32[512,8192]{1,0:T(8,128)S(1)} %add.82), channel_id=1, source_target_pairs={{0,4},{1,5},{2,6},{3,7},{4,0},{5,1},{6,2},{7,3},{8,12},{9,13},{10,... | collective-permute-start | bytes 50331656 | tf_op jit(solution)/shard_map/ppermute | solution.py:76
  1182.3 373.3 %copy-start.5 = (f32[8192]{0:T(1024)S(1)}, f32[8192]{0:T(1024)}, u32[]{:S(2)}) copy-start(f32[8192]{0:T(1024)} %param.12) | copy-start | bytes 98308
  1182.3 361.3 %collective-permute-start.5 = (f32[512,8192]{1,0:T(8,128)}, f32[512,8192]{1,0:T(8,128)S(1)}, u32[]{:S(2)}, u32[]{:S(2)}) collective-permute-start(f32[512,8192]{1,0:T(8,128)} %add.83), channel_id=1, source_target_pairs={{0,8},{1,9},{2,10},{3,11},{4,12},{5,13},{6,14},{7,15},{8,0},{9,1},... | collective-permute-start | bytes 50331656 | tf_op jit(solution)/shard_map/ppermute | solution.py:76
  1571.2 54.8 %all-gather.7.cloned.1.call-start = ((), (), s32[]{:S(2)}) async-start(), calls=%async_computation.1 | async-start | bytes 2359296 | tf_op jit(solution)/shard_map/all_gather | solution.py:94
  1603.7 5.7 copy-start
Sparse Core Ops, SparseCore 0:
  1571.3 27.1 all-gather.4
  1600.1 25.7 all-gather.6
